TPU v7x, 32 devices: a whole 2x2x4 slice. The times are simulated.
32 devices in a mesh: grp: 1, head: 16 (over z, x, core), tile: 2 (over y).
Axes of the slice: x: 2, y: 2, z: 4, core: 2. Of those that a mesh axis runs over, the one named last changes fastest.
Arguments:
- attention: bfloat16 [144, 256, 256], P(('grp', 'head'), None, 'tile'), may hold values from 0 to 16, as said below
- proj_weight: bfloat16 [64, 144], replicated, may hold values from -0.5 to 0.5
- proj_bias: float32 [64], replicated, may hold values from -1.8 to 1.8
- conv_weight: bfloat16 [2, 2, 64, 64, 3, 3], replicated, may hold values from -0.25 to 0.25
- conv_bias: float32 [2, 2, 64], replicated, may hold values from -1.8 to 1.8
- out_weight: float32 [64], replicated, may hold values from -0.75 to 0.75
Outputs:
- logits: float32 [256, 256], P(('grp', 'head'), 'tile')
Inputs may be any that keep to these rules, and one draw needn't show every extreme that they name: `attention`: every entry is positive.
All inputs are finite; a program needn't handle non-finite values.
Results may differ from a plain program's by a relative error of at most 0.007.
Values may be sent and summed in bfloat16 or wider, within the bound.
A program may use at most 128 MiB of HBM per device.

v0:
```python
import jax
import jax.numpy as jnp
from jax import lax
from jax.sharding import PartitionSpec as P


def extended(cells, sides, width):
    for axis, dim in sides:
        count = lax.axis_size(axis)
        ends = count - 1
        head = lax.slice_in_dim(cells, 0, width, axis=dim)
        tail = lax.slice_in_dim(cells, cells.shape[dim] - width, cells.shape[dim], axis=dim)
        cells = jnp.concatenate(
            [
                lax.ppermute(tail, axis, [(i, (i + 1) % count) for i in range(ends)]),
                cells,
                lax.ppermute(head, axis, [((i + 1) % count, i) for i in range(ends)]),
            ],
            axis=dim,
        )
    return cells


def convolve(padded, kernel, offsets):
    result = lax.conv_general_dilated(
        padded[None], kernel, (1, 1), "VALID", preferred_element_type=jnp.float32
    )[0]
    return result + offsets[:, None, None]


def with_edges(field):
    banded = extended(field, ((("head", "tile"), 1),), 1)
    return jnp.pad(banded, ((0, 0), (0, 0), (1, 1)))


def on_device(attention, proj_weight, proj_bias, conv_weight, conv_bias, out_weight):
    columns = attention.shape[2]
    offset = lax.axis_index("tile") * columns
    swapped = lax.all_to_all(attention, "tile", split_axis=1, concat_axis=2, tiled=True)
    mirror = jnp.swapaxes(swapped, 1, 2)
    symmetric = attention.astype(jnp.float32) + mirror.astype(jnp.float32)
    column_part = jnp.sum(symmetric, axis=1)
    rowsum = lax.all_gather(column_part, "tile", axis=1, tiled=True)
    grand_total = jnp.sum(rowsum, axis=1)
    symmetric = attention.astype(jnp.float32) + mirror.astype(jnp.float32)
    own_totals = lax.dynamic_slice_in_dim(rowsum, offset, columns, 1)
    corrected = (
        symmetric - rowsum[:, :, None] * own_totals[:, None, :] / grand_total[:, None, None]
    ).astype(jnp.bfloat16)
    grouped = lax.all_to_all(
        lax.all_to_all(corrected, "head", split_axis=1, concat_axis=0, tiled=True),
        "tile",
        split_axis=1,
        concat_axis=2,
        tiled=True,
    )
    stream = jnp.einsum("kc,crs->krs", proj_weight, grouped, preferred_element_type=jnp.float32)
    stream = (stream + proj_bias[:, None, None]).astype(jnp.bfloat16)
    for layer_index in range(conv_weight.shape[0]):
        hidden = jax.nn.elu(
            convolve(with_edges(stream), conv_weight[layer_index, 0], conv_bias[layer_index, 0])
        ).astype(jnp.bfloat16)
        update = convolve(
            with_edges(hidden), conv_weight[layer_index, 1], conv_bias[layer_index, 1]
        )
        stream = (stream.astype(jnp.float32) + update).astype(jnp.bfloat16)
    logits = jnp.einsum(
        "k,krs->rs", out_weight, stream.astype(jnp.float32), precision=lax.Precision.HIGHEST
    )
    logits = lax.all_to_all(
        logits.astype(jnp.bfloat16), "tile", split_axis=1, concat_axis=0, tiled=True
    ).astype(logits.dtype)
    return logits


def solution(mesh):
    return jax.shard_map(
        on_device,
        mesh=mesh,
        in_specs=(P(("grp", "head"), None, "tile"), P(), P(), P(), P(), P()),
        out_specs=P(("grp", "head"), "tile"),
        check_vma=False,
    )
```

profile of v0, /device:TPU:0, one launch (start us, length us, event | category | flops | bytes accessed | tf_op | source)
XLA Modules:
  0.0 138.6 jit_solution(11967543169565332876)
XLA Ops:
  0.0 2.5 %copy.55 = bf16[9,256,128]{2,0,1:T(8,128)(2,1)} copy(bf16[9,256,128]{2,1,0:T(8,128)(2,1)} %param.6) | data formatting | bytes 1179648 | tf_op args[0]
  2.5 4.3 %all-to-all-start = ((bf16[9,256,128]{2,0,1:T(8,128)(2,1)}), bf16[9,256,128]{2,0,1:T(8,128)(2,1)S(1)}, u32[]{:S(2)}, u32[]{:S(2)}) async-start(bf16[9,256,128]{2,0,1:T(8,128)(2,1)} %copy.55), calls=%async_computation | async-start | bytes 2097152 | tf_op jit(solution)/shard_map/all_to_all | solution.py:39
  6.7 14.4 %all-to-all-done = bf16[9,256,128]{2,0,1:T(8,128)(2,1)S(1)} async-done(((bf16[9,256,128]{2,0,1:T(8,128)(2,1)}), bf16[9,256,128]{2,0,1:T(8,128)(2,1)S(1)}, u32[]{:S(2)}, u32[]{:S(2)}) %all-to-all-start) | async-done | bytes 589856 | tf_op jit(solution)/shard_map/all_to_all | solution.py:39
  21.2 1.5 %convert_bitcast_fusion = f32[9,128,2,128]{3,0,1,2:T(8,128)} fusion(bf16[9,2,128,128]{3,0,2,1:T(8,128)(2,1)S(1)} %bitcast.140), kind=kLoop, calls=%fused_computation.5 | loop fusion | flops 294912 | bytes 1769472 | tf_op jit(solution)/shard_map/convert_element_type | solution.py:45
  22.7 2.6 %copy.57 = f32[9,128,2,128]{1,0,3,2:T(8,128)S(1)} copy(f32[9,128,2,128]{3,0,1,2:T(8,128)} %convert_bitcast_fusion) | data formatting | bytes 2359296 | tf_op jit(solution)/shard_map/convert_element_type | solution.py:45
  25.8 4.4 %all_gather.3 = f32[9,256]{1,0:T(8,128)S(1)} all-gather(f32[9,128]{1,0:T(8,128)S(1)} %fusion), channel_id=1, replica_groups=mesh['grp'=1,'head'=16,'tile'=2] {'tile'}, dimensions={1}, use_global_device_ids=true | all-gather | bytes 13824 | tf_op jit(solution)/shard_map/all_gather | solution.py:43
  31.4 30.6 %all_to_all.58 = bf16[9,256,128]{2,0,1:T(8,128)(2,1)S(1)} all-to-all(bf16[9,256,128]{2,0,1:T(8,128)(2,1)S(1)} %subtract_convert_fusion), channel_id=1, replica_groups=mesh['grp'=1,'head'=16,'tile'=2] {'head'}, dimensions={1} | all-to-all | bytes 1179648 | tf_op jit(solution)/shard_map/all_to_all | solution.py:51
  62.4 12.5 %all_to_all.59 = bf16[144,16,128]{2,0,1:T(8,128)(2,1)S(1)} all-to-all(bf16[144,16,128]{2,0,1:T(8,128)(2,1)S(1)} %copy.61), channel_id=1, replica_groups=mesh['grp'=1,'head'=16,'tile'=2] {'tile'}, dimensions={1} | all-to-all | bytes 1179648 | tf_op jit(solution)/shard_map/all_to_all | solution.py:50
  75.2 1.3 collective-permute-start.1
  76.5 4.5 %collective-permute-start = (bf16[64,1,256]{2,0,1:T(8,128)(2,1)S(1)}, bf16[64,1,256]{2,0,1:T(8,128)(2,1)S(1)}, u32[]{:S(2)}, u32[]{:S(2)}) collective-permute-start(bf16[64,1,256]{2,0,1:T(8,128)(2,1)S(1)} %get-tuple-element.11), channel_id=1, source_target_pairs={{0,1},{1,2},{2,3},{3,4},{4,5},{5,6},{6,7},{7,8},{8,9},{9,10},{10,1... | collective-permute-start | bytes 98312 | tf_op jit(solution)/shard_map/ppermute | solution.py:15
  81.0 1.5 %collective-permute-done = bf16[64,1,256]{2,0,1:T(8,128)(2,1)S(1)} collective-permute-done((bf16[64,1,256]{2,0,1:T(8,128)(2,1)S(1)}, bf16[64,1,256]{2,0,1:T(8,128)(2,1)S(1)}, u32[]{:S(2)}, u32[]{:S(2)}) %collective-permute-start) | collective-permute-done | bytes 32800 | tf_op jit(solution)/shard_map/ppermute | solution.py:15
  85.1 1.4 %convolution_select_fusion.3 = f32[8,8,33,64]{3,1,2,0:T(8,128)S(1)} fusion(bf16[64,10,1,7,2]{0,3,4,1,2:T(8,128)(2,1)S(1)} %slice.74, bf16[64,10,1,8,33]{0,3,4,1,2:T(8,128)(2,1)S(1)} %copy.66, pred[8,33]{0,1:T(8,128)(4,1)S(1)} %copy-done.6, bf16[2,2,64,64,3,3]{3,2,5,4,1,0:T(8,128)(2,1)S(1)} %copy-done.4), kind=kOutput, calls=%fused_computation.18 | convolution fusion | flops 156923904 | bytes 1410048 | tf_op jit(solution)/shard_map/conv_general_dilated | solution.py:25
  87.4 1.3 collective-permute-start.3
  88.7 4.9 %collective-permute-start.2 = (bf16[64,1,256]{0,1,2:T(2,128)(2,1)S(1)}, bf16[64,1,256]{0,1,2:T(2,128)(2,1)S(1)}, u32[]{:S(2)}, u32[]{:S(2)}) collective-permute-start(bf16[64,1,256]{0,1,2:T(2,128)(2,1)S(1)} %get-tuple-element.7), channel_id=1, source_target_pairs={{0,1},{1,2},{2,3},{3,4},{4,5},{5,6},{6,7},{7,8},{8,9},{9,10},{10,1... | collective-permute-start | bytes 98312 | tf_op jit(solution)/shard_map/ppermute | solution.py:15
  94.9 2.5 %collective-permute-done.2 = bf16[64,1,256]{0,1,2:T(2,128)(2,1)S(1)} collective-permute-done((bf16[64,1,256]{0,1,2:T(2,128)(2,1)S(1)}, bf16[64,1,256]{0,1,2:T(2,128)(2,1)S(1)}, u32[]{:S(2)}, u32[]{:S(2)}) %collective-permute-start.2) | collective-permute-done | bytes 32800 | tf_op jit(solution)/shard_map/ppermute | solution.py:15
  100.0 1.4 %convolution_select_fusion.2 = f32[8,8,33,64]{3,1,2,0:T(8,128)S(1)} fusion(bf16[64,10,1,7,2]{0,3,4,1,2:T(8,128)(2,1)S(1)} %slice.78, bf16[64,10,1,8,33]{0,3,4,1,2:T(8,128)(2,1)S(1)} %copy.73, pred[8,33]{0,1:T(8,128)(4,1)S(1)} %copy-done.6, bf16[2,2,64,64,3,3]{3,2,5,4,1,0:T(8,128)(2,1)S(1)} %copy-done.4), kind=kOutput, calls=%fused_computation.17 | convolution fusion | flops 156923904 | bytes 1410048 | tf_op jit(solution)/shard_map/conv_general_dilated | solution.py:25
  103.6 5.2 %collective-permute-start.4 = (bf16[64,1,256]{2,0,1:T(8,128)(2,1)S(1)}, bf16[64,1,256]{2,0,1:T(8,128)(2,1)S(1)}, u32[]{:S(2)}, u32[]{:S(2)}) collective-permute-start(bf16[64,1,256]{2,0,1:T(8,128)(2,1)S(1)} %get-tuple-element.9), channel_id=1, source_target_pairs={{0,1},{1,2},{2,3},{3,4},{4,5},{5,6},{6,7},{7,8},{8,9},{9,10},{10,1... | collective-permute-start | bytes 98312 | tf_op jit(solution)/shard_map/ppermute | solution.py:15
  108.8 1.4 %collective-permute-done.4 = bf16[64,1,256]{2,0,1:T(8,128)(2,1)S(1)} collective-permute-done((bf16[64,1,256]{2,0,1:T(8,128)(2,1)S(1)}, bf16[64,1,256]{2,0,1:T(8,128)(2,1)S(1)}, u32[]{:S(2)}, u32[]{:S(2)}) %collective-permute-start.4) | collective-permute-done | bytes 32800 | tf_op jit(solution)/shard_map/ppermute | solution.py:15
  112.6 1.4 %convolution_select_fusion.1 = f32[8,8,33,64]{3,1,2,0:T(8,128)S(1)} fusion(bf16[64,10,1,7,2]{0,3,4,1,2:T(8,128)(2,1)S(1)} %slice.82, bf16[64,10,1,8,33]{0,3,4,1,2:T(8,128)(2,1)S(1)} %copy.78, pred[8,33]{0,1:T(8,128)(4,1)S(1)} %copy-done.6, bf16[2,2,64,64,3,3]{3,2,5,4,1,0:T(8,128)(2,1)S(1)} %copy-done.4), kind=kOutput, calls=%fused_computation.16 | convolution fusion | flops 156923904 | bytes 1410048 | tf_op jit(solution)/shard_map/conv_general_dilated | solution.py:25
  116.2 4.9 %collective-permute-start.6 = (bf16[64,1,256]{0,1,2:T(2,128)(2,1)S(1)}, bf16[64,1,256]{0,1,2:T(2,128)(2,1)S(1)}, u32[]{:S(2)}, u32[]{:S(2)}) collective-permute-start(bf16[64,1,256]{0,1,2:T(2,128)(2,1)S(1)} %get-tuple-element.5), channel_id=1, source_target_pairs={{0,1},{1,2},{2,3},{3,4},{4,5},{5,6},{6,7},{7,8},{8,9},{9,10},{10,1... | collective-permute-start | bytes 98312 | tf_op jit(solution)/shard_map/ppermute | solution.py:15
  121.4 1.5 %collective-permute-done.7 = bf16[64,1,256]{0,1,2:T(2,128)(2,1)S(1)} collective-permute-done((bf16[64,1,256]{0,1,2:T(2,128)(2,1)S(1)}, bf16[64,1,256]{0,1,2:T(2,128)(2,1)S(1)}, u32[]{:S(2)}, u32[]{:S(2)}) %collective-permute-start.7) | collective-permute-done | bytes 32800 | tf_op jit(solution)/shard_map/ppermute | solution.py:17
  123.0 2.4 %collective-permute-done.6 = bf16[64,1,256]{0,1,2:T(2,128)(2,1)S(1)} collective-permute-done((bf16[64,1,256]{0,1,2:T(2,128)(2,1)S(1)}, bf16[64,1,256]{0,1,2:T(2,128)(2,1)S(1)}, u32[]{:S(2)}, u32[]{:S(2)}) %collective-permute-start.6) | collective-permute-done | bytes 32800 | tf_op jit(solution)/shard_map/ppermute | solution.py:15
  128.0 1.4 %convolution_select_fusion = f32[8,8,33,64]{3,1,2,0:T(8,128)S(1)} fusion(bf16[64,10,1,7,2]{0,3,4,1,2:T(8,128)(2,1)S(1)} %slice.86, bf16[64,10,1,8,33]{0,3,4,1,2:T(8,128)(2,1)S(1)} %copy.85, pred[8,33]{0,1:T(8,128)(4,1)S(1)} %copy-done.6, bf16[2,2,64,64,3,3]{3,2,5,4,1,0:T(8,128)(2,1)S(1)} %copy-done.4), kind=kOutput, calls=%fused_computation.15 | convolution fusion | flops 156923904 | bytes 1410048 | tf_op jit(solution)/shard_map/conv_general_dilated | solution.py:25
  130.6 7.3 %all_to_all.60 = bf16[8,2,128]{2,0,1:T(8,128)(2,1)S(1)} all-to-all(bf16[8,2,128]{2,0,1:T(8,128)(2,1)S(1)} %bitcast.144), channel_id=1, replica_groups=mesh['grp'=1,'head'=16,'tile'=2] {'tile'}, dimensions={1} | all-to-all | bytes 8192 | tf_op jit(solution)/shard_map/all_to_all | solution.py:70
  (72 shorter events, 20.9 us)
Async XLA Ops:
  0.0 74.9 %copy-start = (bf16[64,144]{1,0:T(8,128)(2,1)S(1)}, bf16[64,144]{1,0:T(8,128)(2,1)}, u32[]{:S(2)}) copy-start(bf16[64,144]{1,0:T(8,128)(2,1)} %param.7) | copy-start | bytes 55300
  2.5 18.7 %all-to-all-start = ((bf16[9,256,128]{2,0,1:T(8,128)(2,1)}), bf16[9,256,128]{2,0,1:T(8,128)(2,1)S(1)}, u32[]{:S(2)}, u32[]{:S(2)}) async-start(bf16[9,256,128]{2,0,1:T(8,128)(2,1)} %copy.55), calls=%async_computation | async-start | bytes 2097152 | tf_op jit(solution)/shard_map/all_to_all | solution.py:39
  22.7 2.6 %copy-start.1 = (bf16[9,256,128]{2,1,0:T(8,128)(2,1)S(1)}, bf16[9,256,128]{2,1,0:T(8,128)(2,1)}, u32[]{:S(2)}) copy-start(bf16[9,256,128]{2,1,0:T(8,128)(2,1)} %param.6) | copy-start | bytes 1769476
  62.2 12.7 %copy-start.5 = (f32[64]{0:T(128)S(1)}, f32[64]{0:T(128)}, u32[]{:S(2)}) copy-start(f32[64]{0:T(128)} %param.8) | copy-start | bytes 772
  62.2 18.8 %copy-start.2 = (f32[2,2,64]{2,1,0:T(2,128)S(1)}, f32[2,2,64]{2,1,0:T(2,128)}, u32[]{:S(2)}) copy-start(f32[2,2,64]{2,1,0:T(2,128)} %param.10) | copy-start | bytes 3076
  75.2 5.9 %collective-permute-start.1 = (bf16[64,1,256]{2,0,1:T(8,128)(2,1)S(1)}, bf16[64,1,256]{2,0,1:T(8,128)(2,1)S(1)}, u32[]{:S(2)}, u32[]{:S(2)}) collective-permute-start(bf16[64,1,256]{2,0,1:T(8,128)(2,1)S(1)} %get-tuple-element.12), channel_id=1, source_target_pairs={{1,0},{2,1},{3,2},{4,3},{5,4},{6,5},{7,6},{8,7},{9,8},{10,9},{11,1... | collective-permute-start | bytes 98312 | tf_op jit(solution)/shard_map/ppermute | solution.py:17
  76.5 6.1 %collective-permute-start = (bf16[64,1,256]{2,0,1:T(8,128)(2,1)S(1)}, bf16[64,1,256]{2,0,1:T(8,128)(2,1)S(1)}, u32[]{:S(2)}, u32[]{:S(2)}) collective-permute-start(bf16[64,1,256]{2,0,1:T(8,128)(2,1)S(1)} %get-tuple-element.11), channel_id=1, source_target_pairs={{0,1},{1,2},{2,3},{3,4},{4,5},{5,6},{6,7},{7,8},{8,9},{9,10},{10,1... | collective-permute-start | bytes 98312 | tf_op jit(solution)/shard_map/ppermute | solution.py:15
  84.0 1.1 copy-start.4
  84.0 1.1 copy-start.6
  87.4 7.4 %collective-permute-start.3 = (bf16[64,1,256]{0,1,2:T(2,128)(2,1)S(1)}, bf16[64,1,256]{0,1,2:T(2,128)(2,1)S(1)}, u32[]{:S(2)}, u32[]{:S(2)}) collective-permute-start(bf16[64,1,256]{0,1,2:T(2,128)(2,1)S(1)} %get-tuple-element.8), channel_id=1, source_target_pairs={{1,0},{2,1},{3,2},{4,3},{5,4},{6,5},{7,6},{8,7},{9,8},{10,9},{11,1... | collective-permute-start | bytes 98312 | tf_op jit(solution)/shard_map/ppermute | solution.py:17
  88.7 8.7 %collective-permute-start.2 = (bf16[64,1,256]{0,1,2:T(2,128)(2,1)S(1)}, bf16[64,1,256]{0,1,2:T(2,128)(2,1)S(1)}, u32[]{:S(2)}, u32[]{:S(2)}) collective-permute-start(bf16[64,1,256]{0,1,2:T(2,128)(2,1)S(1)} %get-tuple-element.7), channel_id=1, source_target_pairs={{0,1},{1,2},{2,3},{3,4},{4,5},{5,6},{6,7},{7,8},{8,9},{9,10},{10,1... | collective-permute-start | bytes 98312 | tf_op jit(solution)/shard_map/ppermute | solution.py:15
  102.3 6.5 %collective-permute-start.5 = (bf16[64,1,256]{2,0,1:T(8,128)(2,1)S(1)}, bf16[64,1,256]{2,0,1:T(8,128)(2,1)S(1)}, u32[]{:S(2)}, u32[]{:S(2)}) collective-permute-start(bf16[64,1,256]{2,0,1:T(8,128)(2,1)S(1)} %get-tuple-element.10), channel_id=1, source_target_pairs={{1,0},{2,1},{3,2},{4,3},{5,4},{6,5},{7,6},{8,7},{9,8},{10,9},{11,1... | collective-permute-start | bytes 98312 | tf_op jit(solution)/shard_map/ppermute | solution.py:17
  103.6 6.6 %collective-permute-start.4 = (bf16[64,1,256]{2,0,1:T(8,128)(2,1)S(1)}, bf16[64,1,256]{2,0,1:T(8,128)(2,1)S(1)}, u32[]{:S(2)}, u32[]{:S(2)}) collective-permute-start(bf16[64,1,256]{2,0,1:T(8,128)(2,1)S(1)} %get-tuple-element.9), channel_id=1, source_target_pairs={{0,1},{1,2},{2,3},{3,4},{4,5},{5,6},{6,7},{7,8},{8,9},{9,10},{10,1... | collective-permute-start | bytes 98312 | tf_op jit(solution)/shard_map/ppermute | solution.py:15
  114.9 8.0 %collective-permute-start.7 = (bf16[64,1,256]{0,1,2:T(2,128)(2,1)S(1)}, bf16[64,1,256]{0,1,2:T(2,128)(2,1)S(1)}, u32[]{:S(2)}, u32[]{:S(2)}) collective-permute-start(bf16[64,1,256]{0,1,2:T(2,128)(2,1)S(1)} %get-tuple-element.6), channel_id=1, source_target_pairs={{1,0},{2,1},{3,2},{4,3},{5,4},{6,5},{7,6},{8,7},{9,8},{10,9},{11,1... | collective-permute-start | bytes 98312 | tf_op jit(solution)/shard_map/ppermute | solution.py:17
  116.2 9.2 %collective-permute-start.6 = (bf16[64,1,256]{0,1,2:T(2,128)(2,1)S(1)}, bf16[64,1,256]{0,1,2:T(2,128)(2,1)S(1)}, u32[]{:S(2)}, u32[]{:S(2)}) collective-permute-start(bf16[64,1,256]{0,1,2:T(2,128)(2,1)S(1)} %get-tuple-element.5), channel_id=1, source_target_pairs={{0,1},{1,2},{2,3},{3,4},{4,5},{5,6},{6,7},{7,8},{8,9},{9,10},{10,1... | collective-permute-start | bytes 98312 | tf_op jit(solution)/shard_map/ppermute | solution.py:15
  129.7 0.7 copy-start.3
where the time goes:
time: 140 us; the launch traced here: 139 us
  blocking collectives  54.8 us (39%)
  starting transfers between devices  28.9 us (21%)
  waiting for transfers between devices  24.7 us (18%)
  local copies, waits for them, and re-layouts  17.6 us (13%)
  matrix products  6.19 us (4%)
  other arithmetic  5.83 us (4%)
    all_to_all x1, blocking collectives, on_device(): lax.all_to_all(corrected, 'head', split_axis=1, concat_axis=0, tiled=True)  30.6 us
    ppermute x4, starting transfers between devices, extended(): lax.ppermute(tail, axis, [(i, (i + 1) % count) for i in range(ends)])  19.5 us
    all_to_all x1, waiting for transfers between devices, on_device(): lax.all_to_all(attention, 'tile', split_axis=1, concat_axis=2, tiled=True)  14.4 us
    all_to_all x1, blocking collectives, on_device(): lax.all_to_all(lax.all_to_all(corrected, 'head', split_axis=1, concat_axi...  12.5 us
    conv_general_dilated x18, local copies, waits for them, and re-layouts, convolve(): lax.conv_general_dilated(padded[None], kernel, (1, 1), 'VALID', preferred...  9.49 us
    ppermute x4, waiting for transfers between devices, extended(): lax.ppermute(tail, axis, [(i, (i + 1) % count) for i in range(ends)])  7.87 us
    all_to_all x1, blocking collectives, on_device(): lax.all_to_all(logits.astype(jnp.bfloat16), 'tile', split_axis=1, concat_...  7.34 us
    conv_general_dilated x4, matrix products, convolve(): lax.conv_general_dilated(padded[None], kernel, (1, 1), 'VALID', preferred...  5.66 us
  transfers between devices with their start and end apart: 9, of which 7 were waited for; matrix products, arithmetic and copies ran while one was open for 1% of the time, Pallas kernels for 0%

commit v1 on v0

v1 whole, which is shorter than its diff:
```python
import functools
import jax
import jax.numpy as jnp
from jax import lax
from jax.experimental import pallas as pl
from jax.experimental.pallas import tpu as pltpu
from jax.sharding import PartitionSpec as P

VM = pltpu.VMEM


def remote(src, dst, send, recv, head, tile):
    return pltpu.make_async_remote_copy(
        src_ref=src,
        dst_ref=dst,
        send_sem=send,
        recv_sem=recv,
        device_id={"head": head, "tile": tile},
        device_id_type=pl.DeviceIdType.MESH,
    )


def signal(sem, head, tile):
    pl.semaphore_signal(
        sem, inc=1, device_id={"head": head, "tile": tile},
        device_id_type=pl.DeviceIdType.MESH,
    )


def spread_kernel(
    nh, nt, chunks, a_ref, g_ref, mirror, own, parts, corr,
    msend, mrecv, psend, precv, gsend, grecv, lsem,
):
    maps, width, cols = a_ref.shape
    band = g_ref.shape[2]
    per = maps // chunks
    bands = cols // band
    nd = nh * nt
    h = lax.axis_index("head")
    t = lax.axis_index("tile")
    me = h * nt + t
    barrier = pltpu.get_barrier_semaphore()

    def greet(k, _):
        d = lax.rem(me + k, nd)
        signal(barrier, d // nt, lax.rem(d, nt))
        return 0

    lax.fori_loop(1, nd, greet, 0)

    ones_t = jnp.ones((8, cols), jnp.bfloat16)
    ones_w = jnp.ones((8, width), jnp.bfloat16)

    def partial_sums(c, _):
        a = a_ref[c]
        rows = lax.dot_general(
            ones_t, a, (((1,), (1,)), ((), ())), preferred_element_type=jnp.float32
        )
        own[c] = rows
        columns = jnp.dot(ones_w, a, preferred_element_type=jnp.float32)
        at = pl.ds(pl.multiple_of(t * cols, cols), cols)
        own[c, :, at] = own[c, :, at] + columns
        return 0

    def mirror_copy(k, q):
        p = lax.rem(t + k, nt)
        return remote(
            a_ref.at[pl.ds(q * per, per), pl.ds(pl.multiple_of(p * cols, cols), cols), :],
            mirror.at[t, pl.ds(q * per, per)],
            msend.at[q, k - 1], mrecv.at[q, k - 1], h, p,
        )

    def parts_copy(k):
        p = lax.rem(t + k, nt)
        return remote(own, parts.at[k - 1], psend.at[k - 1], precv.at[k - 1], h, p)

    pl.semaphore_wait(barrier, nd - 1)
    for q in range(chunks):
        for k in range(1, nt):
            mirror_copy(k, q).start()
    lax.fori_loop(0, maps, partial_sums, 0)
    for k in range(1, nt):
        parts_copy(k).start()
    for k in range(1, nt):
        parts_copy(k).wait()

    for q in range(chunks):
        for k in range(1, nt):
            mirror_copy(k, q).wait()

        def one_map(c, _):
            sums = own[c]
            for k in range(1, nt):
                sums = sums + parts[k - 1, c]
            own[c] = sums
            total = jnp.sum(sums[0:1], axis=1, keepdims=True)
            at = pl.ds(pl.multiple_of(t * cols, cols), cols)
            scaled = own[c, 0:1, at] / total
            for p in range(nt):
                rows = pl.ds(p * cols, cols)
                block = jnp.where(p == t, a_ref[c, rows, :], mirror[p, c])
                sym = a_ref[c, rows, :].astype(jnp.float32) + block.astype(jnp.float32).T
                r = jnp.broadcast_to(own[c, 0:1, rows], (cols, cols)).T
                value = (sym - r * scaled).astype(jnp.bfloat16)
                corr[q, pl.ds(p * bands, bands), c - q * per] = value.reshape(bands, band, cols)
            return 0

        lax.fori_loop(q * per, (q + 1) * per, one_map, 0)

        def ship(k, _):
            d = lax.rem(me + k, nd)
            remote(
                corr.at[q, d], g_ref.at[me, pl.ds(q * per, per)],
                gsend, grecv, d // nt, lax.rem(d, nt),
            ).start()
            return 0

        lax.fori_loop(1, nd, ship, 0)
        pltpu.make_async_copy(corr.at[q, me], g_ref.at[me, pl.ds(q * per, per)], lsem.at[q]).start()

    for q in range(chunks):
        pltpu.make_async_copy(corr.at[q, me], g_ref.at[me, pl.ds(q * per, per)], lsem.at[q]).wait()
    rest = g_ref.at[pl.ds(0, nd - 1)]
    pltpu.make_async_copy(rest, rest, gsend).wait()
    pltpu.make_async_copy(rest, rest, grecv).wait()


def spread(attention):
    nh, nt = lax.axis_size("head"), lax.axis_size("tile")
    nd = nh * nt
    maps, width, cols = attention.shape
    chunks = 3 if maps % 3 == 0 else 1
    band = width // nd
    far = max(nt - 1, 1)
    return pl.pallas_call(
        functools.partial(spread_kernel, nh, nt, chunks),
        out_shape=jax.ShapeDtypeStruct((nd, maps, band, cols), jnp.bfloat16),
        in_specs=[pl.BlockSpec(memory_space=VM)],
        out_specs=pl.BlockSpec(memory_space=VM),
        scratch_shapes=[
            VM((nt, maps, cols, cols), jnp.bfloat16),
            VM((maps, 8, width), jnp.float32),
            VM((far, maps, 8, width), jnp.float32),
            VM((chunks, nd, maps // chunks, band, cols), jnp.bfloat16),
            pltpu.SemaphoreType.DMA((chunks, far)),
            pltpu.SemaphoreType.DMA((chunks, far)),
            pltpu.SemaphoreType.DMA((far,)),
            pltpu.SemaphoreType.DMA((far,)),
            pltpu.SemaphoreType.DMA,
            pltpu.SemaphoreType.DMA,
            pltpu.SemaphoreType.DMA((chunks,)),
        ],
        compiler_params=pltpu.CompilerParams(
            collective_id=0, has_side_effects=True, vmem_limit_bytes=48 * 1024 * 1024
        ),
        name="spread",
    )(attention)


def stack_kernel(
    nh, nt, x_ref, pw_ref, pb_ref, cw_ref, cb_ref, ow_ref, out_ref,
    stream, hidden, taps, logits, hsend, hrecv, lsend, lrecv, csem,
):
    band, maps, width = x_ref.shape
    feat = pw_ref.shape[0]
    layers = cw_ref.shape[0]
    halo = 2 * layers
    rows = band + 2 * halo
    nd = nh * nt
    h = lax.axis_index("head")
    t = lax.axis_index("tile")
    me = h * nt + t
    up = lax.rem(me + nd - 1, nd)
    down = lax.rem(me + 1, nd)
    barrier = pltpu.get_barrier_semaphore()
    signal(barrier, up // nt, lax.rem(up, nt))
    signal(barrier, down // nt, lax.rem(down, nt))
    for k in range(1, nt):
        signal(barrier, h, lax.rem(t + k, nt))

    def project(r, _):
        value = jnp.dot(pw_ref[...], x_ref[r], preferred_element_type=jnp.float32)
        stream[halo + r] = (value + pb_ref[...]).astype(jnp.bfloat16)
        return 0

    lax.fori_loop(0, band, project, 0)
    pl.semaphore_wait(barrier, nt + 1)

    to_up = remote(
        stream.at[pl.ds(halo, halo)], stream.at[pl.ds(halo + band, halo)],
        hsend.at[0], hrecv.at[0], up // nt, lax.rem(up, nt),
    )
    to_down = remote(
        stream.at[pl.ds(band, halo)], stream.at[pl.ds(0, halo)],
        hsend.at[1], hrecv.at[1], down // nt, lax.rem(down, nt),
    )
    to_up.start()
    to_down.start()
    to_up.wait()
    to_down.wait()

    lane = lax.broadcasted_iota(jnp.int32, (feat, width), 1)
    first = me * band - halo

    def tap(source, dim, r, inside):
        v = source[r].astype(jnp.float32)
        if inside:
            g = first + r
            keep = jnp.logical_and(g >= 0, g < nd * band)
            v = jnp.where(keep, v, 0.0)
        before = jnp.where(lane == 0, 0.0, pltpu.roll(v, 1, 1))
        after = jnp.where(lane == width - 1, 0.0, pltpu.roll(v, width - 1, 1))
        stacked = jnp.concatenate(
            [before.astype(jnp.bfloat16), v.astype(jnp.bfloat16), after.astype(jnp.bfloat16)], axis=0
        )
        taps[r] = jnp.dot(cw_ref[dim[0], dim[1]], stacked, preferred_element_type=jnp.float32)

    for layer in range(layers):
        for half in range(2):
            low = 2 * layer + half
            source = hidden if half else stream

            def taps_of(r, _, source=source, layer=layer, half=half):
                tap(source, (layer, half), r, True)
                return 0

            lax.fori_loop(low, rows - low, taps_of, 0)

            def gather(r, _, layer=layer, half=half):
                conv = (
                    taps[r - 1, 0:feat] + taps[r, feat : 2 * feat] + taps[r + 1, 2 * feat :]
                    + cb_ref[layer, half]
                )
                if half:
                    stream[r] = (stream[r].astype(jnp.float32) + conv).astype(jnp.bfloat16)
                else:
                    hidden[r] = jnp.where(
                        conv > 0.0, conv, jnp.exp(jnp.minimum(conv, 0.0)) - 1.0
                    ).astype(jnp.bfloat16)
                return 0

            lax.fori_loop(low + 1, rows - low - 1, gather, 0)

    cols = width // nt
    for r in range(band):
        line = jnp.sum(stream[halo + r].astype(jnp.float32) * ow_ref[...], axis=0, keepdims=True)
        for p in range(nt):
            logits[p, r : r + 1, :] = line[:, p * cols : (p + 1) * cols]

    def deliver(k):
        p = lax.rem(t + k, nt)
        return remote(
            logits.at[p], out_ref.at[t], lsend.at[k - 1], lrecv.at[k - 1], h, p,
        )

    for k in range(1, nt):
        deliver(k).start()
    keep = pltpu.make_async_copy(logits.at[t], out_ref.at[t], csem)
    keep.start()
    keep.wait()
    for k in range(1, nt):
        deliver(k).wait()


def stack(x, pw, pb, cw, cb, ow):
    nh, nt = lax.axis_size("head"), lax.axis_size("tile")
    band, maps, width = x.shape
    feat = pw.shape[0]
    rows = band + 4 * cw.shape[0]
    far = max(nt - 1, 1)
    return pl.pallas_call(
        functools.partial(stack_kernel, nh, nt),
        out_shape=jax.ShapeDtypeStruct((nt, band, width // nt), jnp.float32),
        in_specs=[pl.BlockSpec(memory_space=VM)] * 6,
        out_specs=pl.BlockSpec(memory_space=VM),
        scratch_shapes=[
            VM((rows, feat, width), jnp.bfloat16),
            VM((rows, feat, width), jnp.bfloat16),
            VM((rows, 3 * feat, width), jnp.float32),
            VM((nt, band, width // nt), jnp.float32),
            pltpu.SemaphoreType.DMA((2,)),
            pltpu.SemaphoreType.DMA((2,)),
            pltpu.SemaphoreType.DMA((far,)),
            pltpu.SemaphoreType.DMA((far,)),
            pltpu.SemaphoreType.DMA,
        ],
        compiler_params=pltpu.CompilerParams(
            collective_id=1, has_side_effects=True, vmem_limit_bytes=48 * 1024 * 1024
        ),
        name="stack",
    )(x, pw, pb, cw, cb, ow)


def on_device(attention, proj_weight, proj_bias, conv_weight, conv_bias, out_weight):
    nh, nt = lax.axis_size("head"), lax.axis_size("tile")
    maps, width, cols = attention.shape
    grouped = spread(attention)
    band = grouped.shape[2]
    grouped = grouped.reshape(nh, nt, maps, band, cols)
    x = jnp.transpose(grouped, (3, 0, 2, 1, 4)).reshape(band, nh * maps, width)
    layers, two, feat = conv_weight.shape[:3]
    cw = jnp.transpose(conv_weight, (0, 1, 4, 2, 5, 3)).reshape(layers, two, 3 * feat, 3 * feat)
    out = stack(
        x, proj_weight, proj_bias[:, None], cw, conv_bias[..., None], out_weight[:, None]
    )
    return out.reshape(nt * band, cols)


def solution(mesh):
    return jax.shard_map(
        on_device,
        mesh=mesh,
        in_specs=(P(("grp", "head"), None, "tile"), P(), P(), P(), P(), P()),
        out_specs=P(("grp", "head"), "tile"),
        check_vma=False,
    )
```

time: 140 us -> 64.7 us (0.46)
  Pallas kernels: 0 us -> 58.3 us
  blocking collectives: 54.8 us -> 0 us
  starting transfers between devices: 28.9 us -> 0 us
  waiting for transfers between devices: 24.7 us -> 0 us
  local copies, waits for them, and re-layouts: 17.6 us -> 5.98 us
  matrix products: 6.19 us -> 0 us
  other arithmetic: 5.83 us -> 0 us
    pallas_call x0 -> x2, Pallas kernels: none -> 58.3 us  [the longest x1 30 us: spread(): pl.pallas_call(functools.partial(spread_kernel, nh, nt, chunks), out_shap...]
    all_to_all x3 -> x0, blocking collectives: 50.5 us -> none  [the longest x1 30.6 us: on_device(): lax.all_to_all(corrected, 'head', split_axis=1, concat_axis=0, tiled=True)]
    ppermute x8 -> x0, starting transfers between devices: 24.6 us -> none  [the longest x4 19.5 us: extended(): lax.ppermute(tail, axis, [(i, (i + 1) % count) for i in range(ends)])]
    all_to_all x1 -> x0, waiting for transfers between devices: 14.4 us -> none  [on_device(): lax.all_to_all(attention, 'tile', split_axis=1, concat_axis=2, tiled=True)]
    ppermute x8 -> x0, waiting for transfers between devices: 10.3 us -> none  [the longest x4 7.87 us: extended(): lax.ppermute(tail, axis, [(i, (i + 1) % count) for i in range(ends)])]
    conv_general_dilated x18 -> x0, local copies, waits for them, and re-layouts: 9.49 us -> none  [convolve(): lax.conv_general_dilated(padded[None], kernel, (1, 1), 'VALID', preferred...]
    conv_general_dilated x4 -> x0, matrix products: 5.66 us -> none  [convolve(): lax.conv_general_dilated(padded[None], kernel, (1, 1), 'VALID', preferred...]
    all_gather x1 -> x0, blocking collectives: 4.36 us -> none  [on_device(): rowsum = lax.all_gather(column_part, 'tile', axis=1, tiled=True)]
  transfers between devices with their start and end apart: 9 -> 0, of which waited for: 7 -> 0; matrix products, arithmetic and copies ran while one was open for 1% -> 0% of each run, Pallas kernels for 0% -> 0%
where the time goes in v1:
time: 64.7 us; the launch traced here: 64.4 us
  Pallas kernels  58.3 us (90%)
  local copies, waits for them, and re-layouts  5.98 us (9%)
    pallas_call x1, Pallas kernels, spread(): pl.pallas_call(functools.partial(spread_kernel, nh, nt, chunks), out_shap...  30 us
    pallas_call x1, Pallas kernels, stack(): pl.pallas_call(functools.partial(stack_kernel, nh, nt), out_shape=jax.Sha...  28.3 us
    unnamed x13, local copies, waits for them, and re-layouts  3.88 us

profile of v1, /device:TPU:0, one launch (start us, length us, event | category | flops | bytes accessed | tf_op | source)
XLA Modules:
  0.0 64.4 jit_solution(18133895813824029914)
XLA Ops:
  0.0 0.0 copy-start
  0.0 1.1 %copy-done = bf16[9,256,128]{2,1,0:T(8,128)(2,1)S(1)} copy-done((bf16[9,256,128]{2,1,0:T(8,128)(2,1)S(1)}, bf16[9,256,128]{2,1,0:T(8,128)(2,1)}, u32[]{:S(2)}) %copy-start) | copy-done | bytes 589848
  1.1 30.0 %spread.1 = bf16[32,9,8,128]{3,2,1,0:T(8,128)(2,1)S(1)} custom-call(bf16[9,256,128]{2,1,0:T(8,128)(2,1)S(1)} %copy-done), custom_call_target="tpu_custom_call" | custom-call | tf_op jit(solution)/shard_map/spread/pallas_call | solution.py:135
  31.1 0.5 copy.17
  31.6 0.0 copy-start.2
  31.6 0.4 reshape.13.x_ref
  32.0 0.7 %copy-done.2 = bf16[2,2,64,64,3,3]{3,2,5,4,1,0:T(8,128)(2,1)S(1)} copy-done((bf16[2,2,64,64,3,3]{3,2,5,4,1,0:T(8,128)(2,1)S(1)}, bf16[2,2,64,64,3,3]{3,2,5,4,1,0:T(8,128)(2,1)}, u32[]{:S(2)}) %copy-start.2) | copy-done | bytes 294936
  32.6 0.5 copy.12
  33.2 0.0 copy-start.3
  33.2 0.4 reshape.14.cw_ref
  33.6 0.2 copy-done.3
  33.8 0.1 copy.14.cb_ref
  34.0 0.0 copy-start.4
  34.0 0.7 %copy-done.4 = f32[64]{0:T(128)S(1)} copy-done((f32[64]{0:T(128)S(1)}, f32[64]{0:T(128)}, u32[]{:S(2)}) %copy-start.4) | copy-done | bytes 280
  34.6 0.0 copy-start.1
  34.6 0.1 copy.13.pb_ref
  34.7 0.0 copy-start.5
  34.7 0.7 %copy-done.5 = f32[64]{0:T(128)S(1)} copy-done((f32[64]{0:T(128)S(1)}, f32[64]{0:T(128)}, u32[]{:S(2)}) %copy-start.5) | copy-done | bytes 280
  35.4 0.1 copy.15.ow_ref
  35.5 0.0 copy-done.1
  35.5 28.3 %stack.1 = f32[2,8,128]{2,1,0:T(8,128)S(1)} custom-call(bf16[8,144,256]{2,1,0:T(8,128)(2,1)S(1)} %reshape.13.x_ref, bf16[64,144]{1,0:T(8,128)(2,1)S(1)} %copy-done.1, f32[64,1]{1,0:T(8,128)S(1)} %copy.13.pb_ref, bf16[2,2,192,192]{3,2,1,0:T(8,128)(2,1)S(1)} %reshape.14.cw_ref, f32[2,2,64,1]{3,2,1,0:T(8,128)S(1)} %copy.14.cb_ref, f32[64,1]{1,0:T(8,128)S(1)} %copy.15.ow_ref), custom_call_target="tpu_custom_call" | custom-call | tf_op jit(solution)/shard_map/stack/pallas_call | solution.py:271
  63.8 0.6 copy.19
Async XLA Ops:
  0.0 1.1 %copy-start = (bf16[9,256,128]{2,1,0:T(8,128)(2,1)S(1)}, bf16[9,256,128]{2,1,0:T(8,128)(2,1)}, u32[]{:S(2)}) copy-start(bf16[9,256,128]{2,1,0:T(8,128)(2,1)} %a_ref.1) | copy-start | bytes 1769476
  31.6 1.1 %copy-start.2 = (bf16[2,2,64,64,3,3]{3,2,5,4,1,0:T(8,128)(2,1)S(1)}, bf16[2,2,64,64,3,3]{3,2,5,4,1,0:T(8,128)(2,1)}, u32[]{:S(2)}) copy-start(bf16[2,2,64,64,3,3]{3,2,5,4,1,0:T(8,128)(2,1)} %param.9) | copy-start | bytes 884740
  33.2 0.7 %copy-start.3 = (f32[2,2,64]{2,1,0:T(2,128)S(1)}, f32[2,2,64]{2,1,0:T(2,128)}, u32[]{:S(2)}) copy-start(f32[2,2,64]{2,1,0:T(2,128)} %param.10) | copy-start | bytes 3076
  34.0 0.7 %copy-start.4 = (f32[64]{0:T(128)S(1)}, f32[64]{0:T(128)}, u32[]{:S(2)}) copy-start(f32[64]{0:T(128)} %param.8) | copy-start | bytes 772
  34.6 0.9 %copy-start.1 = (bf16[64,144]{1,0:T(8,128)(2,1)S(1)}, bf16[64,144]{1,0:T(8,128)(2,1)}, u32[]{:S(2)}) copy-start(bf16[64,144]{1,0:T(8,128)(2,1)} %pw_ref.1) | copy-start | bytes 55300
  34.7 0.7 %copy-start.5 = (f32[64]{0:T(128)S(1)}, f32[64]{0:T(128)}, u32[]{:S(2)}) copy-start(f32[64]{0:T(128)} %param.11) | copy-start | bytes 772

commit v2 on v0

v2 whole, which is shorter than its diff:
```python
import functools
import jax
import jax.numpy as jnp
from jax import lax
from jax.experimental import pallas as pl
from jax.experimental.pallas import tpu as pltpu
from jax.sharding import PartitionSpec as P

VM = pltpu.VMEM
GROUP = 4


def remote(src, dst, send, recv, head, tile):
    return pltpu.make_async_remote_copy(
        src_ref=src,
        dst_ref=dst,
        send_sem=send,
        recv_sem=recv,
        device_id={"head": head, "tile": tile},
        device_id_type=pl.DeviceIdType.MESH,
    )


def sweep(low, high, body):
    groups = (high - low) // GROUP

    def step(i, _):
        body(low + i * GROUP, GROUP)
        return 0

    if groups:
        lax.fori_loop(0, groups, step, 0)
    if low + groups * GROUP < high:
        body(low + groups * GROUP, high - low - groups * GROUP)


def kernel(
    nh, nt, chunks, a_hbm, pw_ref, pb_ref, cw_hbm, cb_ref, ow_ref, out_ref,
    a_ref, cw_ref, mirror, own, parts, corr, got, wide, weights, stream, hidden, taps, logits,
    asem, wsem, msend, mrecv, psend, precv, gsend, grecv, lsem,
    hsend, hrecv, osend, orecv, csem,
):
    maps, width, cols = a_ref.shape
    band = got.shape[2]
    per = maps // chunks
    bands = cols // band
    nd = nh * nt
    feat = pw_ref.shape[0]
    layers = cw_ref.shape[0]
    halo = 2 * layers
    rows = band + 2 * halo
    h = lax.axis_index("head")
    t = lax.axis_index("tile")
    me = h * nt + t
    up = lax.rem(me + nd - 1, nd)
    down = lax.rem(me + 1, nd)

    load = pltpu.make_async_copy(a_hbm, a_ref, asem)
    load.start()
    load_weights = pltpu.make_async_copy(cw_hbm, cw_ref, wsem)
    load_weights.start()
    barrier = pltpu.get_barrier_semaphore()

    def greet(k, _):
        d = lax.rem(me + k, nd)
        pl.semaphore_signal(
            barrier, inc=1, device_id={"head": d // nt, "tile": lax.rem(d, nt)},
            device_id_type=pl.DeviceIdType.MESH,
        )
        return 0

    lax.fori_loop(1, nd, greet, 0)
    load.wait()
    mine = pl.ds(pl.multiple_of(t * cols, cols), cols)
    ones_t = jnp.ones((8, cols), jnp.bfloat16)
    ones_w = jnp.ones((8, width), jnp.bfloat16)

    def mirror_copy(k, q):
        p = lax.rem(t + k, nt)
        return remote(
            a_ref.at[pl.ds(q * per, per), pl.ds(pl.multiple_of(p * cols, cols), cols), :],
            mirror.at[t, pl.ds(q * per, per)],
            msend.at[q, k - 1], mrecv.at[q, k - 1], h, p,
        )

    def parts_copy(k):
        p = lax.rem(t + k, nt)
        return remote(own, parts.at[k - 1], psend.at[k - 1], precv.at[k - 1], h, p)

    def partial_sums(i, _):
        for j in range(per):
            c = i * per + j
            a = a_ref[c]
            line = lax.dot_general(
                ones_t, a, (((1,), (1,)), ((), ())), preferred_element_type=jnp.float32
            )
            own[c] = line
            columns = jnp.dot(ones_w, a, preferred_element_type=jnp.float32)
            own[c, :, mine] = own[c, :, mine] + columns
            mirror[t, c] = a_ref[c, mine, :]
        return 0

    pl.semaphore_wait(barrier, nd - 1)
    for q in range(chunks):
        for k in range(1, nt):
            mirror_copy(k, q).start()
    lax.fori_loop(0, chunks, partial_sums, 0)
    for k in range(1, nt):
        parts_copy(k).start()

    load_weights.wait()
    for layer in range(layers):
        for half in range(2):
            for dy in range(3):
                weights[layer, half, dy * feat : (dy + 1) * feat, :] = jnp.concatenate(
                    [cw_ref[layer, half, dy, dx].astype(jnp.float32) for dx in range(3)], axis=1
                ).astype(jnp.bfloat16)

    for k in range(1, nt):
        parts_copy(k).wait()

    for q in range(chunks):
        for k in range(1, nt):
            mirror_copy(k, q).wait()

        def one_map(c, slot, q=q):
            sums = own[c]
            for k in range(1, nt):
                sums = sums + parts[k - 1, c]
            own[c] = sums
            total = jnp.sum(sums, axis=1, keepdims=True)
            scaled = (own[c, :, mine] / total).T[:, 0:1]
            for p in range(nt):
                at = pl.ds(p * cols, cols)
                turned = mirror[p, c].astype(jnp.float32) - scaled * own[c, 0:1, at]
                value = (a_ref[c, at, :].astype(jnp.float32) + turned.T).astype(jnp.bfloat16)
                corr[q, pl.ds(p * bands, bands), slot] = value.reshape(bands, band, cols)

        for j in range(per):
            one_map(q * per + j, j)

        def ship(k, _, q=q):
            d = lax.rem(me + k, nd)
            remote(
                corr.at[q, d], got.at[me, pl.ds(q * per, per)],
                gsend, grecv, d // nt, lax.rem(d, nt),
            ).start()
            return 0

        lax.fori_loop(1, nd, ship, 0)
        pltpu.make_async_copy(corr.at[q, me], got.at[me, pl.ds(q * per, per)], lsem.at[q]).start()

    for q in range(chunks):
        pltpu.make_async_copy(corr.at[q, me], got.at[me, pl.ds(q * per, per)], lsem.at[q]).wait()
    rest = got.at[pl.ds(0, nd - 1)]
    pltpu.make_async_copy(rest, rest, grecv).wait()

    def unpack(i, _):
        for p in range(nt):
            wide[p, pl.ds(i * maps * band, maps * band), :] = (
                got[i * nt + p].astype(jnp.float32).reshape(maps * band, cols)
            )
        return 0

    lax.fori_loop(0, nh, unpack, 0)
    for r in range(band):
        x = jnp.concatenate(
            [wide[p, pl.ds(r, nh * maps, stride=band), :] for p in range(nt)], axis=1
        ).astype(jnp.bfloat16)
        value = jnp.dot(pw_ref[...], x, preferred_element_type=jnp.float32)
        stream[halo + r] = (value + pb_ref[...]).astype(jnp.bfloat16)

    to_up = remote(
        stream.at[pl.ds(halo, halo)], stream.at[pl.ds(halo + band, halo)],
        hsend.at[0], hrecv.at[0], up // nt, lax.rem(up, nt),
    )
    to_down = remote(
        stream.at[pl.ds(band, halo)], stream.at[pl.ds(0, halo)],
        hsend.at[1], hrecv.at[1], down // nt, lax.rem(down, nt),
    )
    to_up.start()
    to_down.start()

    lane = lax.broadcasted_iota(jnp.int32, (feat, width), 1)
    first = me * band - halo

    def taps_of(source, layer, half):
        def body(r, count):
            pieces = []
            for j in range(count):
                g = first + r + j
                keep = jnp.logical_and(g >= 0, g < nd * band)
                v = jnp.where(keep, source[r + j].astype(jnp.float32), 0.0)
                before = jnp.where(lane == 0, 0.0, pltpu.roll(v, 1, 1))
                after = jnp.where(lane == width - 1, 0.0, pltpu.roll(v, width - 1, 1))
                pieces.append(
                    jnp.concatenate(
                        [before.astype(jnp.bfloat16), v.astype(jnp.bfloat16), after.astype(jnp.bfloat16)],
                        axis=0,
                    )
                )
            block = jnp.dot(
                weights[layer, half], jnp.concatenate(pieces, axis=1),
                preferred_element_type=jnp.float32,
            )
            for j in range(count):
                taps[r + j] = block[:, j * width : (j + 1) * width]

        return body

    def gather_of(layer, half):
        bias = cb_ref[layer, half]

        def body(r, count):
            for j in range(count):
                s = r + j
                conv = (
                    taps[s - 1, 0:feat] + taps[s, feat : 2 * feat] + taps[s + 1, 2 * feat :] + bias
                )
                if half:
                    stream[s] = (stream[s].astype(jnp.float32) + conv).astype(jnp.bfloat16)
                else:
                    hidden[s] = jnp.where(
                        conv > 0.0, conv, jnp.exp(jnp.minimum(conv, 0.0)) - 1.0
                    ).astype(jnp.bfloat16)

        return body

    for layer in range(layers):
        for half in range(2):
            low = 2 * layer + half
            body = taps_of(hidden if half else stream, layer, half)
            if low:
                sweep(low, rows - low, body)
            else:
                sweep(halo, halo + band, body)
                to_up.wait()
                to_down.wait()
                sweep(0, halo, body)
                sweep(halo + band, rows, body)
            sweep(low + 1, rows - low - 1, gather_of(layer, half))

    for r in range(band):
        line = jnp.sum(stream[halo + r].astype(jnp.float32) * ow_ref[...], axis=0, keepdims=True)
        for p in range(nt):
            logits[p, r : r + 1, :] = line[:, p * cols : (p + 1) * cols]

    def deliver(k):
        p = lax.rem(t + k, nt)
        return remote(
            logits.at[p], out_ref.at[t], osend.at[k - 1], orecv.at[k - 1], h, p,
        )

    for k in range(1, nt):
        deliver(k).start()
    keep_own = pltpu.make_async_copy(logits.at[t], out_ref.at[t], csem)
    keep_own.start()
    keep_own.wait()
    for k in range(1, nt):
        deliver(k).wait()
    pltpu.make_async_copy(rest, rest, gsend).wait()


def on_device(attention, proj_weight, proj_bias, conv_weight, conv_bias, out_weight):
    nh, nt = lax.axis_size("head"), lax.axis_size("tile")
    nd = nh * nt
    maps, width, cols = attention.shape
    layers, two, feat = conv_weight.shape[:3]
    chunks = 3 if maps % 3 == 0 else 1
    band = width // nd
    far = max(nt - 1, 1)
    rows = band + 4 * layers
    ordered = jnp.transpose(conv_weight, (0, 1, 4, 5, 2, 3))
    dma = pltpu.SemaphoreType.DMA
    out = pl.pallas_call(
        functools.partial(kernel, nh, nt, chunks),
        out_shape=jax.ShapeDtypeStruct((nt, band, cols), jnp.float32),
        in_specs=[
            pl.BlockSpec(memory_space=pltpu.HBM),
            pl.BlockSpec(memory_space=VM),
            pl.BlockSpec(memory_space=VM),
            pl.BlockSpec(memory_space=pltpu.HBM),
            pl.BlockSpec(memory_space=VM),
            pl.BlockSpec(memory_space=VM),
        ],
        out_specs=pl.BlockSpec(memory_space=VM),
        scratch_shapes=[
            VM((maps, width, cols), jnp.bfloat16),
            VM(ordered.shape, jnp.bfloat16),
            VM((nt, maps, cols, cols), jnp.bfloat16),
            VM((maps, 8, width), jnp.float32),
            VM((far, maps, 8, width), jnp.float32),
            VM((chunks, nd, maps // chunks, band, cols), jnp.bfloat16),
            VM((nd, maps, band, cols), jnp.bfloat16),
            VM((nt, nh * maps * band, cols), jnp.float32),
            VM((layers, two, 3 * feat, 3 * feat), jnp.bfloat16),
            VM((rows, feat, width), jnp.bfloat16),
            VM((rows, feat, width), jnp.bfloat16),
            VM((rows, 3 * feat, width), jnp.float32),
            VM((nt, band, cols), jnp.float32),
            dma,
            dma,
            dma((chunks, far)),
            dma((chunks, far)),
            dma((far,)),
            dma((far,)),
            dma,
            dma,
            dma((chunks,)),
            dma((2,)),
            dma((2,)),
            dma((far,)),
            dma((far,)),
            dma,
        ],
        compiler_params=pltpu.CompilerParams(
            collective_id=0, has_side_effects=True, vmem_limit_bytes=56 * 1024 * 1024
        ),
        name="head",
    )(
        attention, proj_weight, proj_bias[:, None], ordered, conv_bias[..., None],
        out_weight[:, None],
    )
    return out.reshape(nt * band, cols)


def solution(mesh):
    return jax.shard_map(
        on_device,
        mesh=mesh,
        in_specs=(P(("grp", "head"), None, "tile"), P(), P(), P(), P(), P()),
        out_specs=P(("grp", "head"), "tile"),
        check_vma=False,
    )
```

time: 140 us -> 51.3 us (0.37)
  blocking collectives: 54.8 us -> 0 us
  Pallas kernels: 0 us -> 46.9 us
  starting transfers between devices: 28.9 us -> 0 us
  waiting for transfers between devices: 24.7 us -> 0 us
  local copies, waits for them, and re-layouts: 17.6 us -> 4.15 us
  matrix products: 6.19 us -> 0 us
  other arithmetic: 5.83 us -> 0 us
    all_to_all x3 -> x0, blocking collectives: 50.5 us -> none  [the longest x1 30.6 us: on_device(): lax.all_to_all(corrected, 'head', split_axis=1, concat_axis=0, tiled=True)]
    pallas_call x0 -> x1, Pallas kernels: none -> 46.9 us  [on_device(): pl.pallas_call(functools.partial(kernel, nh, nt, chunks), out_shape=jax.S...]
    ppermute x8 -> x0, starting transfers between devices: 24.6 us -> none  [the longest x4 19.5 us: extended(): lax.ppermute(tail, axis, [(i, (i + 1) % count) for i in range(ends)])]
    all_to_all x1 -> x0, waiting for transfers between devices: 14.4 us -> none  [on_device(): lax.all_to_all(attention, 'tile', split_axis=1, concat_axis=2, tiled=True)]
    ppermute x8 -> x0, waiting for transfers between devices: 10.3 us -> none  [the longest x4 7.87 us: extended(): lax.ppermute(tail, axis, [(i, (i + 1) % count) for i in range(ends)])]
    conv_general_dilated x18 -> x0, local copies, waits for them, and re-layouts: 9.49 us -> none  [convolve(): lax.conv_general_dilated(padded[None], kernel, (1, 1), 'VALID', preferred...]
    conv_general_dilated x4 -> x0, matrix products: 5.66 us -> none  [convolve(): lax.conv_general_dilated(padded[None], kernel, (1, 1), 'VALID', preferred...]
    all_gather x1 -> x0, blocking collectives: 4.36 us -> none  [on_device(): rowsum = lax.all_gather(column_part, 'tile', axis=1, tiled=True)]
  transfers between devices with their start and end apart: 9 -> 0, of which waited for: 7 -> 0; matrix products, arithmetic and copies ran while one was open for 1% -> 0% of each run, Pallas kernels for 0% -> 0%
where the time goes in v2:
time: 51.3 us; the launch traced here: 51 us
  Pallas kernels  46.9 us (91%)
  local copies, waits for them, and re-layouts  4.15 us (8%)
    pallas_call x1, Pallas kernels, on_device(): pl.pallas_call(functools.partial(kernel, nh, nt, chunks), out_shape=jax.S...  46.9 us
    unnamed x7, local copies, waits for them, and re-layouts  1.96 us

profile of v2, /device:TPU:0, one launch (start us, length us, event | category | flops | bytes accessed | tf_op | source)
XLA Modules:
  0.0 51.0 jit_solution(955639426240105832)
XLA Ops:
  0.0 0.0 copy-start.1
  0.0 0.7 %copy-done.1 = f32[64]{0:T(128)S(1)} copy-done((f32[64]{0:T(128)S(1)}, f32[64]{0:T(128)}, u32[]{:S(2)}) %copy-start.1) | copy-done | bytes 280
  0.7 0.0 copy-start.2
  0.7 0.7 %copy.9.pb_ref = f32[64,1]{1,0:T(8,128)} copy(f32[64,1]{0,1:T(1,128)S(1)} %bitcast.8) | data formatting | bytes 512 | tf_op jit(solution)/shard_map/broadcast_in_dim | solution.py:321
  1.4 0.0 copy-done.2
  1.4 0.0 copy-start
  1.4 0.7 %copy.11.ow_ref = f32[64,1]{1,0:T(8,128)} copy(f32[64,1]{0,1:T(1,128)S(1)} %bitcast.9) | data formatting | bytes 512 | tf_op jit(solution)/shard_map/broadcast_in_dim | solution.py:322
  2.1 0.0 copy-done
  2.1 0.8 %copy.10.cb_ref = f32[2,2,64,1]{3,2,1,0:T(8,128)} copy(f32[2,2,64,1]{2,1,0,3:T(2,128)S(1)} %bitcast.7) | data formatting | bytes 2048 | tf_op jit(solution)/shard_map/broadcast_in_dim | solution.py:321
  2.9 46.9 %head.1 = f32[2,8,128]{2,1,0:T(8,128)} custom-call(bf16[9,256,128]{2,1,0:T(8,128)(2,1)} %a_hbm.1, bf16[64,144]{1,0:T(8,128)(2,1)} %pw_ref.1, f32[64,1]{1,0:T(8,128)} %copy.9.pb_ref, bf16[2,2,3,3,64,64]{5,4,3,2,1,0:T(8,128)(2,1)} %bitcast.5, f32[2,2,64,1]{3,2,1,0:T(8,128)} %copy.10.cb_ref, f32[64,1]{1,0:T(8,128)} %copy.11.ow_ref), custom_call_target="tpu_custom_call" | custom-call | tf_op jit(solution)/shard_map/head/pallas_call | solution.py:275
  49.7 1.3 %copy.13 = f32[16,128]{1,0:T(8,128)} copy(f32[16,128]{1,0:T(8,128)} %bitcast.6) | data formatting | bytes 16384
Async XLA Ops:
  0.0 0.7 %copy-start.1 = (f32[64]{0:T(128)S(1)}, f32[64]{0:T(128)}, u32[]{:S(2)}) copy-start(f32[64]{0:T(128)} %param.8) | copy-start | bytes 772
  0.7 0.7 %copy-start.2 = (f32[64]{0:T(128)S(1)}, f32[64]{0:T(128)}, u32[]{:S(2)}) copy-start(f32[64]{0:T(128)} %param.11) | copy-start | bytes 772
  1.4 0.7 %copy-start = (f32[2,2,64]{2,1,0:T(2,128)S(1)}, f32[2,2,64]{2,1,0:T(2,128)}, u32[]{:S(2)}) copy-start(f32[2,2,64]{2,1,0:T(2,128)} %param.10) | copy-start | bytes 3076

commit v3 on v2

--- a/solution.py
+++ b/solution.py
@@ -21,6 +21,20 @@
     )
 
 
+def band_of(head, tile, nt):
+    block, core = head // 2, lax.rem(head, 2)
+    u = jnp.where(lax.rem(block, 2) == 0, tile, nt - 1 - tile)
+    core = jnp.where(lax.rem(u, 2) == 0, core, 1 - core)
+    return block * (2 * nt) + 2 * u + core
+
+
+def place_of(band, nt):
+    block, spot = band // (2 * nt), lax.rem(band, 2 * nt)
+    u, core = spot // 2, lax.rem(spot, 2)
+    core = jnp.where(lax.rem(u, 2) == 0, core, 1 - core)
+    return block * 2 + core, jnp.where(lax.rem(block, 2) == 0, u, nt - 1 - u)
+
+
 def sweep(low, high, body):
     groups = (high - low) // GROUP
 
@@ -36,9 +50,9 @@
 
 def kernel(
     nh, nt, chunks, a_hbm, pw_ref, pb_ref, cw_hbm, cb_ref, ow_ref, out_ref,
-    a_ref, cw_ref, mirror, own, parts, corr, got, wide, weights, stream, hidden, taps, logits,
+    a_ref, cw_ref, mirror, own, total_of, parts, corr, got, wide, weights, stream, hidden, taps, logits,
     asem, wsem, msend, mrecv, psend, precv, gsend, grecv, lsem,
-    hsend, hrecv, osend, orecv, csem,
+    hsend, hrecv, osend, orecv,
 ):
     maps, width, cols = a_ref.shape
     band = got.shape[2]
@@ -52,8 +66,9 @@
     h = lax.axis_index("head")
     t = lax.axis_index("tile")
     me = h * nt + t
-    up = lax.rem(me + nd - 1, nd)
-    down = lax.rem(me + 1, nd)
+    spot = band_of(h, t, nt)
+    up_head, up_tile = place_of(lax.rem(spot + nd - 1, nd), nt)
+    down_head, down_tile = place_of(lax.rem(spot + 1, nd), nt)
 
     load = pltpu.make_async_copy(a_hbm, a_ref, asem)
     load.start()
@@ -61,15 +76,24 @@
     load_weights.start()
     barrier = pltpu.get_barrier_semaphore()
 
-    def greet(k, _):
-        d = lax.rem(me + k, nd)
+    def others(visit):
+        def step(i, _):
+            head = lax.rem(h + i, nh)
+            for k in range(nt):
+                visit(head, lax.rem(t + k, nt))
+            return 0
+
+        for k in range(1, nt):
+            visit(h, lax.rem(t + k, nt))
+        lax.fori_loop(1, nh, step, 0)
+
+    def greet(head, tile):
         pl.semaphore_signal(
-            barrier, inc=1, device_id={"head": d // nt, "tile": lax.rem(d, nt)},
+            barrier, inc=1, device_id={"head": head, "tile": tile},
             device_id_type=pl.DeviceIdType.MESH,
         )
-        return 0
-
-    lax.fori_loop(1, nd, greet, 0)
+
+    others(greet)
     load.wait()
     mine = pl.ds(pl.multiple_of(t * cols, cols), cols)
     ones_t = jnp.ones((8, cols), jnp.bfloat16)
@@ -94,19 +118,16 @@
             line = lax.dot_general(
                 ones_t, a, (((1,), (1,)), ((), ())), preferred_element_type=jnp.float32
             )
-            own[c] = line
+            own[c] = line[0:1]
             columns = jnp.dot(ones_w, a, preferred_element_type=jnp.float32)
-            own[c, :, mine] = own[c, :, mine] + columns
+            own[c, :, mine] = own[c, :, mine] + columns[0:1]
             mirror[t, c] = a_ref[c, mine, :]
         return 0
 
-    pl.semaphore_wait(barrier, nd - 1)
-    for q in range(chunks):
-        for k in range(1, nt):
-            mirror_copy(k, q).start()
     lax.fori_loop(0, chunks, partial_sums, 0)
-    for k in range(1, nt):
-        parts_copy(k).start()
+
+    def upright(line):
+        return jnp.broadcast_to(line, (8, feat)).T[:, 0:1]
 
     load_weights.wait()
     for layer in range(layers):
@@ -116,6 +137,12 @@
                     [cw_ref[layer, half, dy, dx].astype(jnp.float32) for dx in range(3)], axis=1
                 ).astype(jnp.bfloat16)
 
+    pl.semaphore_wait(barrier, nd - 1)
+    for k in range(1, nt):
+        parts_copy(k).start()
+    for q in range(chunks):
+        for k in range(1, nt):
+            mirror_copy(k, q).start()
     for k in range(1, nt):
         parts_copy(k).wait()
 
@@ -127,31 +154,29 @@
             sums = own[c]
             for k in range(1, nt):
                 sums = sums + parts[k - 1, c]
-            own[c] = sums
+            total_of[c] = sums
             total = jnp.sum(sums, axis=1, keepdims=True)
-            scaled = (own[c, :, mine] / total).T[:, 0:1]
+            scaled = jnp.broadcast_to(total_of[c, :, mine] / total, (8, cols)).T[:, 0:1]
             for p in range(nt):
                 at = pl.ds(p * cols, cols)
-                turned = mirror[p, c].astype(jnp.float32) - scaled * own[c, 0:1, at]
+                turned = mirror[p, c].astype(jnp.float32) - scaled * total_of[c, :, at]
                 value = (a_ref[c, at, :].astype(jnp.float32) + turned.T).astype(jnp.bfloat16)
                 corr[q, pl.ds(p * bands, bands), slot] = value.reshape(bands, band, cols)
 
         for j in range(per):
             one_map(q * per + j, j)
 
-        def ship(k, _, q=q):
-            d = lax.rem(me + k, nd)
+        def ship(head, tile, q=q):
             remote(
-                corr.at[q, d], got.at[me, pl.ds(q * per, per)],
-                gsend, grecv, d // nt, lax.rem(d, nt),
+                corr.at[q, band_of(head, tile, nt)], got.at[me, pl.ds(q * per, per)],
+                gsend, grecv, head, tile,
             ).start()
-            return 0
-
-        lax.fori_loop(1, nd, ship, 0)
-        pltpu.make_async_copy(corr.at[q, me], got.at[me, pl.ds(q * per, per)], lsem.at[q]).start()
+
+        others(ship)
+        pltpu.make_async_copy(corr.at[q, spot], got.at[me, pl.ds(q * per, per)], lsem.at[q]).start()
 
     for q in range(chunks):
-        pltpu.make_async_copy(corr.at[q, me], got.at[me, pl.ds(q * per, per)], lsem.at[q]).wait()
+        pltpu.make_async_copy(corr.at[q, spot], got.at[me, pl.ds(q * per, per)], lsem.at[q]).wait()
     rest = got.at[pl.ds(0, nd - 1)]
     pltpu.make_async_copy(rest, rest, grecv).wait()
 
@@ -163,26 +188,27 @@
         return 0
 
     lax.fori_loop(0, nh, unpack, 0)
+    proj_bias = upright(pb_ref[...])
     for r in range(band):
         x = jnp.concatenate(
             [wide[p, pl.ds(r, nh * maps, stride=band), :] for p in range(nt)], axis=1
         ).astype(jnp.bfloat16)
         value = jnp.dot(pw_ref[...], x, preferred_element_type=jnp.float32)
-        stream[halo + r] = (value + pb_ref[...]).astype(jnp.bfloat16)
+        stream[halo + r] = (value + proj_bias).astype(jnp.bfloat16)
 
     to_up = remote(
         stream.at[pl.ds(halo, halo)], stream.at[pl.ds(halo + band, halo)],
-        hsend.at[0], hrecv.at[0], up // nt, lax.rem(up, nt),
+        hsend.at[0], hrecv.at[0], up_head, up_tile,
     )
     to_down = remote(
         stream.at[pl.ds(band, halo)], stream.at[pl.ds(0, halo)],
-        hsend.at[1], hrecv.at[1], down // nt, lax.rem(down, nt),
+        hsend.at[1], hrecv.at[1], down_head, down_tile,
     )
     to_up.start()
     to_down.start()
 
     lane = lax.broadcasted_iota(jnp.int32, (feat, width), 1)
-    first = me * band - halo
+    first = spot * band - halo
 
     def taps_of(source, layer, half):
         def body(r, count):
@@ -209,7 +235,7 @@
         return body
 
     def gather_of(layer, half):
-        bias = cb_ref[layer, half]
+        bias = upright(cb_ref[layer, half : half + 1, :])
 
         def body(r, count):
             for j in range(count):
@@ -240,24 +266,36 @@
                 sweep(halo + band, rows, body)
             sweep(low + 1, rows - low - 1, gather_of(layer, half))
 
+    readout = upright(ow_ref[...])
     for r in range(band):
-        line = jnp.sum(stream[halo + r].astype(jnp.float32) * ow_ref[...], axis=0, keepdims=True)
+        line = jnp.sum(stream[halo + r].astype(jnp.float32) * readout, axis=0, keepdims=True)
         for p in range(nt):
             logits[p, r : r + 1, :] = line[:, p * cols : (p + 1) * cols]
+
+    owner, slot = spot // nt, lax.rem(spot, nt)
 
     def deliver(k):
         p = lax.rem(t + k, nt)
         return remote(
-            logits.at[p], out_ref.at[t], osend.at[k - 1], orecv.at[k - 1], h, p,
+            logits.at[p], out_ref.at[slot], osend.at[k], orecv.at[slot], owner, p,
         )
 
     for k in range(1, nt):
         deliver(k).start()
-    keep_own = pltpu.make_async_copy(logits.at[t], out_ref.at[t], csem)
-    keep_own.start()
-    keep_own.wait()
+
+    @pl.when(owner == h)
+    def _():
+        pltpu.make_async_copy(logits.at[t], out_ref.at[slot], orecv.at[slot]).start()
+
+    @pl.when(owner != h)
+    def _():
+        deliver(0).start()
+        deliver(0).wait_send()
+
     for k in range(1, nt):
-        deliver(k).wait()
+        deliver(k).wait_send()
+    for k in range(nt):
+        pltpu.make_async_copy(logits.at[k], out_ref.at[k], orecv.at[k]).wait()
     pltpu.make_async_copy(rest, rest, gsend).wait()
 
 
@@ -266,7 +304,7 @@
     nd = nh * nt
     maps, width, cols = attention.shape
     layers, two, feat = conv_weight.shape[:3]
-    chunks = 3 if maps % 3 == 0 else 1
+    chunks = maps
     band = width // nd
     far = max(nt - 1, 1)
     rows = band + 4 * layers
@@ -288,8 +326,9 @@
             VM((maps, width, cols), jnp.bfloat16),
             VM(ordered.shape, jnp.bfloat16),
             VM((nt, maps, cols, cols), jnp.bfloat16),
-            VM((maps, 8, width), jnp.float32),
-            VM((far, maps, 8, width), jnp.float32),
+            VM((maps, 1, width), jnp.float32),
+            VM((maps, 1, width), jnp.float32),
+            VM((far, maps, 1, width), jnp.float32),
             VM((chunks, nd, maps // chunks, band, cols), jnp.bfloat16),
             VM((nd, maps, band, cols), jnp.bfloat16),
             VM((nt, nh * maps * band, cols), jnp.float32),
@@ -309,17 +348,15 @@
             dma((chunks,)),
             dma((2,)),
             dma((2,)),
-            dma((far,)),
-            dma((far,)),
-            dma,
+            dma((nt,)),
+            dma((nt,)),
         ],
         compiler_params=pltpu.CompilerParams(
             collective_id=0, has_side_effects=True, vmem_limit_bytes=56 * 1024 * 1024
         ),
         name="head",
     )(
-        attention, proj_weight, proj_bias[:, None], ordered, conv_bias[..., None],
-        out_weight[:, None],
+        attention, proj_weight, proj_bias[None], ordered, conv_bias, out_weight[None],
     )
     return out.reshape(nt * band, cols)
 

time: 51.3 us -> 41.5 us (0.81)
  Pallas kernels: 46.9 us -> 39.9 us
  local copies, waits for them, and re-layouts: 4.15 us -> 1.3 us
    pallas_call x1, Pallas kernels: 46.9 us -> 39.9 us  [on_device(): pl.pallas_call(functools.partial(kernel, nh, nt, chunks), out_shape=jax.S...]
    broadcast_in_dim x3 -> x0, local copies, waits for them, and re-layouts: 2.19 us -> none  [the longest x1 0.77 us: on_device(): conv_bias[..., None]]
    unnamed x7 -> x1, local copies, waits for them, and re-layouts: 1.96 us -> 1.3 us
where the time goes in v3:
time: 41.5 us; the launch traced here: 41.2 us
  Pallas kernels  39.9 us (96%)
  local copies, waits for them, and re-layouts  1.3 us (3%)
    pallas_call x1, Pallas kernels, on_device(): pl.pallas_call(functools.partial(kernel, nh, nt, chunks), out_shape=jax.S...  39.9 us
    unnamed x1, local copies, waits for them, and re-layouts  1.3 us

profile of v3, /device:TPU:0, one launch (start us, length us, event | category | flops | bytes accessed | tf_op | source)
XLA Modules:
  0.0 41.2 jit_solution(1588354908658847822)
XLA Ops:
  0.0 39.9 %head.1 = f32[2,8,128]{2,1,0:T(8,128)} custom-call(bf16[9,256,128]{2,1,0:T(8,128)(2,1)} %a_hbm.1, bf16[64,144]{1,0:T(8,128)(2,1)} %pw_ref.1, f32[1,64]{1,0:T(1,128)} %bitcast.6, bf16[2,2,3,3,64,64]{5,4,3,2,1,0:T(8,128)(2,1)} %bitcast.4, f32[2,2,64]{2,1,0:T(2,128)} %cb_ref.1, f32[1,64]{1,0:T(1,128)} %bitcast.7), custom_call_target="tpu_custom_call" | custom-call | tf_op jit(solution)/shard_map/head/pallas_call | solution.py:313
  39.9 1.3 %copy.8 = f32[16,128]{1,0:T(8,128)} copy(f32[16,128]{1,0:T(8,128)} %bitcast.5) | data formatting | bytes 16384
